TPU v7x, 128 devices: a whole 4x4x4 slice. The times are simulated.
128 devices in a mesh: gx: 16 (over x, z), gy: 8 (over y, core).
Axes of the slice: x: 4, y: 4, z: 4, core: 2. Of those that a mesh axis runs over, the one named last changes fastest.
Arguments:
- particles: float32 [4, 262144], P(None, ('gx', 'gy')), may hold values from -1 to 1, as said below
- tree_cells: float32 [10, 1048576], P(None, ('gx', 'gy')), may hold values from -1 to 1, as said below
- let_list: int32 [128, 128, 4], P(('gx', 'gy')), may hold values from 0 to 63
- let_count: int32 [128, 128], P(('gx', 'gy')), may hold values from 1 to 4, as said below
- part_list: int32 [128, 4, 4], P(('gx', 'gy')), may hold values from 0 to 15
- cell_lists: int32 [2048, 16], P(('gx', 'gy')), may hold values from 0 to 575
- near_lists: int32 [2048, 8], P(('gx', 'gy')), may hold values from 0 to 31
Outputs:
- forces: float32 [4, 262144], P(None, ('gx', 'gy'))
Inputs may be any that keep to these rules, and one draw needn't show every extreme that they name: let_count is 4 wherever sender and receiver are at most 2 apart along gx+gy, and between 1 and 4 elsewhere. `particles`: positions lie in [-1, 1], masses are positive. `tree_cells`: centres lie in [-1, 1], masses are positive, the quadrupole is traceless.
All inputs are finite; a program needn't handle non-finite values.
Results may differ from a plain program's by a relative error of at most 0.0003.
Values sent between devices are 32-bit elements; how exact they have to be, the bound alone decides.
A program may use at most 64 MiB of HBM per device.

v0:
```python
import jax
import jax.numpy as jnp
from jax import lax
from jax.sharding import PartitionSpec as P

BLK = 128


SOFTENING = 0.0025
near_offsets = (1, -1, 2, -2)


def from_behind(block, axis, distance):
    devices = range(lax.axis_size(axis))
    route = [(i - distance, i) for i in devices if i - distance in devices]
    return lax.ppermute(block, axis, route)


def cell_tile(targets, source):
    target_x = targets[0][:, None]
    target_y = targets[1][:, None]
    target_z = targets[2][:, None]
    delta_x = target_x - source[0][None, :]
    delta_y = target_y - source[1][None, :]
    delta_z = target_z - source[2][None, :]
    inverse = 1.0 / jnp.sqrt(delta_x * delta_x + delta_y * delta_y + delta_z * delta_z + SOFTENING)
    inv_square = inverse * inverse
    inv_cube = inverse * inv_square
    inv_five = inv_cube * inv_square
    masses = source[3][None, :]
    quad_x = (
        source[4][None, :] * delta_x + source[7][None, :] * delta_y + source[8][None, :] * delta_z
    )
    quad_y = (
        source[7][None, :] * delta_x + source[5][None, :] * delta_y + source[9][None, :] * delta_z
    )
    quad_z = (
        source[8][None, :] * delta_x + source[9][None, :] * delta_y + source[6][None, :] * delta_z
    )
    contracted = delta_x * quad_x + delta_y * quad_y + delta_z * quad_z
    radial = -masses * inv_cube - 2.5 * contracted * inv_five * inv_square
    accel_x = jnp.sum(radial * delta_x + quad_x * inv_five, axis=1)
    accel_y = jnp.sum(radial * delta_y + quad_y * inv_five, axis=1)
    accel_z = jnp.sum(radial * delta_z + quad_z * inv_five, axis=1)
    potential = jnp.sum(-masses * inverse - 0.5 * contracted * inv_five, axis=1)
    return jnp.stack([accel_x, accel_y, accel_z, potential])


def near_tile(targets, source):
    near_x = targets[0][:, None] - source[0][None, :]
    near_y = targets[1][:, None] - source[1][None, :]
    near_z = targets[2][:, None] - source[2][None, :]
    near_inverse = 1.0 / jnp.sqrt(near_x * near_x + near_y * near_y + near_z * near_z + SOFTENING)
    near_masses = source[3][None, :]
    near_radial = -near_masses * near_inverse * near_inverse * near_inverse
    accel_x = jnp.sum(near_radial * near_x, axis=1)
    accel_y = jnp.sum(near_radial * near_y, axis=1)
    accel_z = jnp.sum(near_radial * near_z, axis=1)
    potential = jnp.sum(-near_masses * near_inverse, axis=1)
    return jnp.stack([accel_x, accel_y, accel_z, potential])


def block_forces(target_blocks, cell_pool, near_pool, cell_lists, near_lists):
    cell_batch = jax.vmap(cell_tile)
    near_batch = jax.vmap(near_tile)

    def add_cells(total, column):
        return (total + cell_batch(target_blocks, cell_pool[column]), None)

    def add_near(total, column):
        return (total + near_batch(target_blocks, near_pool[column]), None)

    start = jnp.zeros(target_blocks.shape, jnp.float32)
    total, unused = lax.scan(add_cells, start, jnp.transpose(cell_lists))
    total, unused = lax.scan(add_near, total, jnp.transpose(near_lists))
    return total


def exchange_cells(chosen):
    moved = lax.all_to_all(chosen, ("gx", "gy"), split_axis=0, concat_axis=0, tiled=True)
    return moved


def body(particles, tree_cells, let_list, let_count, part_list, cell_lists, near_lists):
    part_blocks = jnp.transpose(particles.reshape(4, -1, BLK), (1, 0, 2))
    cell_blocks = jnp.transpose(tree_cells.reshape(10, -1, BLK), (1, 0, 2))
    peers = lax.axis_size(("gx", "gy"))
    slot_count = let_list.shape[2]
    live_mask = (
        lax.broadcasted_iota(jnp.int32, (peers, slot_count), 1) < let_count[0][:, None]
    ).astype(jnp.float32)
    chosen = cell_blocks[let_list[0]] * live_mask[:, :, None, None]
    received = exchange_cells(chosen).reshape(-1, 10, BLK)
    cell_pool = jnp.concatenate([cell_blocks, received], axis=0)
    near_parts = [part_blocks]
    for position, offset in enumerate(near_offsets):
        picked = part_blocks[part_list[0, position]]
        near_parts.append(from_behind(picked, ("gx", "gy"), offset))
    near_pool = jnp.concatenate(near_parts, axis=0)
    total = block_forces(part_blocks, cell_pool, near_pool, cell_lists, near_lists)
    return jnp.transpose(total, (1, 0, 2)).reshape(4, -1)


def solution(mesh):
    return jax.shard_map(
        body,
        mesh=mesh,
        in_specs=(
            P(None, ("gx", "gy")),
            P(None, ("gx", "gy")),
            P(("gx", "gy"), None, None),
            P(("gx", "gy"), None),
            P(("gx", "gy"), None, None),
            P(("gx", "gy"), None),
            P(("gx", "gy"), None),
        ),
        out_specs=P(None, ("gx", "gy")),
        check_vma=False,
    )
```

profile of v0, /device:TPU:1, one launch (start us, length us, event | category | flops | bytes accessed | tf_op | source)
XLA Modules:
  0.0 190.4 jit_solution(5571833494294727444)
XLA Ops:
  5.5 4.8 %copy_multiply_fusion = f32[128,4,10,128]{3,1,2,0:T(4,128)} fusion(f32[128,4,10,128]{3,2,1,0:T(8,128)} %bitcast.153, f32[128,4]{1,0:T(8,128)S(1)} %fusion.34), kind=kLoop, calls=%fused_computation.86 | loop fusion | flops 655360 | bytes 5244928 | tf_op jit(solution)/shard_map/mul | solution.py:92
  10.3 11.5 %all-to-all-start = ((f32[128,4,10,128]{3,1,2,0:T(4,128)}), f32[128,4,10,128]{3,1,2,0:T(4,128)S(1)}, u32[]{:S(2)}, u32[]{:S(2)}) async-start(f32[128,4,10,128]{3,1,2,0:T(4,128)} %copy_multiply_fusion), calls=%async_computation | async-start | bytes 5242880 | tf_op jit(solution)/shard_map/all_to_all | solution.py:80
  22.4 3.5 %collective-permute-start = (f32[4,4,128]{2,1,0:T(4,128)S(1)}, f32[4,4,128]{2,1,0:T(4,128)S(1)}, u32[]{:S(2)}, u32[]{:S(2)}) collective-permute-start(f32[4,4,128]{2,1,0:T(4,128)S(1)} %gather_fusion.3), channel_id=1, source_target_pairs={{0,1},{1,2},{2,3},{3,4},{4,5},{5,6},{6,7},{7,8},{8,9},{9,10},{10,1... | collective-permute-start | bytes 24584 | tf_op jit(solution)/shard_map/ppermute | solution.py:16
  29.1 3.1 %collective-permute-start.2 = (f32[4,4,128]{2,1,0:T(4,128)S(1)}, f32[4,4,128]{2,1,0:T(4,128)S(1)}, u32[]{:S(2)}, u32[]{:S(2)}) collective-permute-start(f32[4,4,128]{2,1,0:T(4,128)S(1)} %gather_fusion.5), channel_id=1, source_target_pairs={{0,2},{1,3},{2,4},{3,5},{4,6},{5,7},{6,8},{7,9},{8,10},{9,11},{10,... | collective-permute-start | bytes 24584 | tf_op jit(solution)/shard_map/ppermute | solution.py:16
  34.2 6.5 %collective-permute-done = f32[4,4,128]{2,1,0:T(4,128)S(1)} collective-permute-done((f32[4,4,128]{2,1,0:T(4,128)S(1)}, f32[4,4,128]{2,1,0:T(4,128)S(1)}, u32[]{:S(2)}, u32[]{:S(2)}) %collective-permute-start) | collective-permute-done | bytes 8224 | tf_op jit(solution)/shard_map/ppermute | solution.py:16
  40.7 8.0 %collective-permute-done.1 = f32[4,4,128]{2,1,0:T(4,128)S(1)} collective-permute-done((f32[4,4,128]{2,1,0:T(4,128)S(1)}, f32[4,4,128]{2,1,0:T(4,128)S(1)}, u32[]{:S(2)}, u32[]{:S(2)}) %collective-permute-start.1) | collective-permute-done | bytes 8224 | tf_op jit(solution)/shard_map/ppermute | solution.py:16
  48.7 9.1 %all-to-all-done = f32[128,4,10,128]{3,1,2,0:T(4,128)S(1)} async-done(((f32[128,4,10,128]{3,1,2,0:T(4,128)}), f32[128,4,10,128]{3,1,2,0:T(4,128)S(1)}, u32[]{:S(2)}, u32[]{:S(2)}) %all-to-all-start) | async-done | bytes 2621472 | tf_op jit(solution)/shard_map/all_to_all | solution.py:80
  58.5 3.9 %copy.46 = f32[576,10,128]{2,1,0:T(8,128)} copy(f32[576,10,128]{2,0,1:T(8,128)S(1)} %pad_maximum_fusion) | data formatting | bytes 5898240
  62.4 98.3 %while.22 = (s32[]{:T(128)}, f32[16,4,128]{2,0,1:T(8,128)S(1)}, s32[16,16]{1,0:T(8,128)S(1)}, f32[576,10,128]{2,1,0:T(8,128)}, f32[16,4,128]{2,0,1:T(8,128)S(1)}, /*index=5*/s32[]{:T(128)}, s32[]{:T(128)}) while((s32[]{:T(128)}, f32[16,4,128]{2,0,1:T(8,128)S(1)}, s32[16,16]{1,0:T(8,128)S(1)}, f32[576,10,128]{2,1,0:T(8,128)}, ...), condition=%wide.region_5.6_spmd.clone, body=%wide.region_0.5_spmd.clone.sunk | while | flops 14191667 | bytes 618851 | solution.py:74
  65.4 3.1 %fusion.52 = (f32[16,128]{1,0:T(8,128)S(1)}, f32[16,128]{1,0:T(8,128)S(1)}, f32[16,128]{1,0:T(8,128)S(1)}, f32[16,128]{1,0:T(8,128)S(1)}) fusion(f32[16,128]{1,0:T(8,128)S(1)} %bitcast.170, f32[16,128]{1,0:T(8,128)S(1)} %bitcast.171, f32[16,128]{1,0:T(8,128)S(1)} %bitcast.172, f32[16,128]{1,0:T(8,128)S(1)} %bitcast.173, ...), kind=kLoop, calls=%fused_computation.67.clone.1 | loop fusion | flops 14147584 | bytes 139264 | tf_op jit(solution)/shard_map/while/body/eval_jaxpr/vmap()/reduce_sum | solution.py:42
  71.6 3.1 %fusion.52 = (f32[16,128]{1,0:T(8,128)S(1)}, f32[16,128]{1,0:T(8,128)S(1)}, f32[16,128]{1,0:T(8,128)S(1)}, f32[16,128]{1,0:T(8,128)S(1)}) fusion(f32[16,128]{1,0:T(8,128)S(1)} %bitcast.170, f32[16,128]{1,0:T(8,128)S(1)} %bitcast.171, f32[16,128]{1,0:T(8,128)S(1)} %bitcast.172, f32[16,128]{1,0:T(8,128)S(1)} %bitcast.173, ...), kind=kLoop, calls=%fused_computation.67.clone.1 | loop fusion | flops 14147584 | bytes 139264 | tf_op jit(solution)/shard_map/while/body/eval_jaxpr/vmap()/reduce_sum | solution.py:42
  77.7 3.1 %fusion.52 = (f32[16,128]{1,0:T(8,128)S(1)}, f32[16,128]{1,0:T(8,128)S(1)}, f32[16,128]{1,0:T(8,128)S(1)}, f32[16,128]{1,0:T(8,128)S(1)}) fusion(f32[16,128]{1,0:T(8,128)S(1)} %bitcast.170, f32[16,128]{1,0:T(8,128)S(1)} %bitcast.171, f32[16,128]{1,0:T(8,128)S(1)} %bitcast.172, f32[16,128]{1,0:T(8,128)S(1)} %bitcast.173, ...), kind=kLoop, calls=%fused_computation.67.clone.1 | loop fusion | flops 14147584 | bytes 139264 | tf_op jit(solution)/shard_map/while/body/eval_jaxpr/vmap()/reduce_sum | solution.py:42
  83.9 3.1 %fusion.52 = (f32[16,128]{1,0:T(8,128)S(1)}, f32[16,128]{1,0:T(8,128)S(1)}, f32[16,128]{1,0:T(8,128)S(1)}, f32[16,128]{1,0:T(8,128)S(1)}) fusion(f32[16,128]{1,0:T(8,128)S(1)} %bitcast.170, f32[16,128]{1,0:T(8,128)S(1)} %bitcast.171, f32[16,128]{1,0:T(8,128)S(1)} %bitcast.172, f32[16,128]{1,0:T(8,128)S(1)} %bitcast.173, ...), kind=kLoop, calls=%fused_computation.67.clone.1 | loop fusion | flops 14147584 | bytes 139264 | tf_op jit(solution)/shard_map/while/body/eval_jaxpr/vmap()/reduce_sum | solution.py:42
  90.0 3.1 %fusion.52 = (f32[16,128]{1,0:T(8,128)S(1)}, f32[16,128]{1,0:T(8,128)S(1)}, f32[16,128]{1,0:T(8,128)S(1)}, f32[16,128]{1,0:T(8,128)S(1)}) fusion(f32[16,128]{1,0:T(8,128)S(1)} %bitcast.170, f32[16,128]{1,0:T(8,128)S(1)} %bitcast.171, f32[16,128]{1,0:T(8,128)S(1)} %bitcast.172, f32[16,128]{1,0:T(8,128)S(1)} %bitcast.173, ...), kind=kLoop, calls=%fused_computation.67.clone.1 | loop fusion | flops 14147584 | bytes 139264 | tf_op jit(solution)/shard_map/while/body/eval_jaxpr/vmap()/reduce_sum | solution.py:42
  96.2 3.1 %fusion.52 = (f32[16,128]{1,0:T(8,128)S(1)}, f32[16,128]{1,0:T(8,128)S(1)}, f32[16,128]{1,0:T(8,128)S(1)}, f32[16,128]{1,0:T(8,128)S(1)}) fusion(f32[16,128]{1,0:T(8,128)S(1)} %bitcast.170, f32[16,128]{1,0:T(8,128)S(1)} %bitcast.171, f32[16,128]{1,0:T(8,128)S(1)} %bitcast.172, f32[16,128]{1,0:T(8,128)S(1)} %bitcast.173, ...), kind=kLoop, calls=%fused_computation.67.clone.1 | loop fusion | flops 14147584 | bytes 139264 | tf_op jit(solution)/shard_map/while/body/eval_jaxpr/vmap()/reduce_sum | solution.py:42
  102.3 3.1 %fusion.52 = (f32[16,128]{1,0:T(8,128)S(1)}, f32[16,128]{1,0:T(8,128)S(1)}, f32[16,128]{1,0:T(8,128)S(1)}, f32[16,128]{1,0:T(8,128)S(1)}) fusion(f32[16,128]{1,0:T(8,128)S(1)} %bitcast.170, f32[16,128]{1,0:T(8,128)S(1)} %bitcast.171, f32[16,128]{1,0:T(8,128)S(1)} %bitcast.172, f32[16,128]{1,0:T(8,128)S(1)} %bitcast.173, ...), kind=kLoop, calls=%fused_computation.67.clone.1 | loop fusion | flops 14147584 | bytes 139264 | tf_op jit(solution)/shard_map/while/body/eval_jaxpr/vmap()/reduce_sum | solution.py:42
  108.4 3.1 %fusion.52 = (f32[16,128]{1,0:T(8,128)S(1)}, f32[16,128]{1,0:T(8,128)S(1)}, f32[16,128]{1,0:T(8,128)S(1)}, f32[16,128]{1,0:T(8,128)S(1)}) fusion(f32[16,128]{1,0:T(8,128)S(1)} %bitcast.170, f32[16,128]{1,0:T(8,128)S(1)} %bitcast.171, f32[16,128]{1,0:T(8,128)S(1)} %bitcast.172, f32[16,128]{1,0:T(8,128)S(1)} %bitcast.173, ...), kind=kLoop, calls=%fused_computation.67.clone.1 | loop fusion | flops 14147584 | bytes 139264 | tf_op jit(solution)/shard_map/while/body/eval_jaxpr/vmap()/reduce_sum | solution.py:42
  114.6 3.1 %fusion.52 = (f32[16,128]{1,0:T(8,128)S(1)}, f32[16,128]{1,0:T(8,128)S(1)}, f32[16,128]{1,0:T(8,128)S(1)}, f32[16,128]{1,0:T(8,128)S(1)}) fusion(f32[16,128]{1,0:T(8,128)S(1)} %bitcast.170, f32[16,128]{1,0:T(8,128)S(1)} %bitcast.171, f32[16,128]{1,0:T(8,128)S(1)} %bitcast.172, f32[16,128]{1,0:T(8,128)S(1)} %bitcast.173, ...), kind=kLoop, calls=%fused_computation.67.clone.1 | loop fusion | flops 14147584 | bytes 139264 | tf_op jit(solution)/shard_map/while/body/eval_jaxpr/vmap()/reduce_sum | solution.py:42
  120.7 3.1 %fusion.52 = (f32[16,128]{1,0:T(8,128)S(1)}, f32[16,128]{1,0:T(8,128)S(1)}, f32[16,128]{1,0:T(8,128)S(1)}, f32[16,128]{1,0:T(8,128)S(1)}) fusion(f32[16,128]{1,0:T(8,128)S(1)} %bitcast.170, f32[16,128]{1,0:T(8,128)S(1)} %bitcast.171, f32[16,128]{1,0:T(8,128)S(1)} %bitcast.172, f32[16,128]{1,0:T(8,128)S(1)} %bitcast.173, ...), kind=kLoop, calls=%fused_computation.67.clone.1 | loop fusion | flops 14147584 | bytes 139264 | tf_op jit(solution)/shard_map/while/body/eval_jaxpr/vmap()/reduce_sum | solution.py:42
  126.9 3.1 %fusion.52 = (f32[16,128]{1,0:T(8,128)S(1)}, f32[16,128]{1,0:T(8,128)S(1)}, f32[16,128]{1,0:T(8,128)S(1)}, f32[16,128]{1,0:T(8,128)S(1)}) fusion(f32[16,128]{1,0:T(8,128)S(1)} %bitcast.170, f32[16,128]{1,0:T(8,128)S(1)} %bitcast.171, f32[16,128]{1,0:T(8,128)S(1)} %bitcast.172, f32[16,128]{1,0:T(8,128)S(1)} %bitcast.173, ...), kind=kLoop, calls=%fused_computation.67.clone.1 | loop fusion | flops 14147584 | bytes 139264 | tf_op jit(solution)/shard_map/while/body/eval_jaxpr/vmap()/reduce_sum | solution.py:42
  133.0 3.1 %fusion.52 = (f32[16,128]{1,0:T(8,128)S(1)}, f32[16,128]{1,0:T(8,128)S(1)}, f32[16,128]{1,0:T(8,128)S(1)}, f32[16,128]{1,0:T(8,128)S(1)}) fusion(f32[16,128]{1,0:T(8,128)S(1)} %bitcast.170, f32[16,128]{1,0:T(8,128)S(1)} %bitcast.171, f32[16,128]{1,0:T(8,128)S(1)} %bitcast.172, f32[16,128]{1,0:T(8,128)S(1)} %bitcast.173, ...), kind=kLoop, calls=%fused_computation.67.clone.1 | loop fusion | flops 14147584 | bytes 139264 | tf_op jit(solution)/shard_map/while/body/eval_jaxpr/vmap()/reduce_sum | solution.py:42
  139.2 3.1 %fusion.52 = (f32[16,128]{1,0:T(8,128)S(1)}, f32[16,128]{1,0:T(8,128)S(1)}, f32[16,128]{1,0:T(8,128)S(1)}, f32[16,128]{1,0:T(8,128)S(1)}) fusion(f32[16,128]{1,0:T(8,128)S(1)} %bitcast.170, f32[16,128]{1,0:T(8,128)S(1)} %bitcast.171, f32[16,128]{1,0:T(8,128)S(1)} %bitcast.172, f32[16,128]{1,0:T(8,128)S(1)} %bitcast.173, ...), kind=kLoop, calls=%fused_computation.67.clone.1 | loop fusion | flops 14147584 | bytes 139264 | tf_op jit(solution)/shard_map/while/body/eval_jaxpr/vmap()/reduce_sum | solution.py:42
  145.3 3.1 %fusion.52 = (f32[16,128]{1,0:T(8,128)S(1)}, f32[16,128]{1,0:T(8,128)S(1)}, f32[16,128]{1,0:T(8,128)S(1)}, f32[16,128]{1,0:T(8,128)S(1)}) fusion(f32[16,128]{1,0:T(8,128)S(1)} %bitcast.170, f32[16,128]{1,0:T(8,128)S(1)} %bitcast.171, f32[16,128]{1,0:T(8,128)S(1)} %bitcast.172, f32[16,128]{1,0:T(8,128)S(1)} %bitcast.173, ...), kind=kLoop, calls=%fused_computation.67.clone.1 | loop fusion | flops 14147584 | bytes 139264 | tf_op jit(solution)/shard_map/while/body/eval_jaxpr/vmap()/reduce_sum | solution.py:42
  160.7 29.0 %while.21 = (s32[]{:T(128)}, f32[16,4,128]{2,0,1:T(8,128)S(1)}, f32[16,4,128]{2,0,1:T(8,128)S(1)}, s32[8,16]{1,0:T(8,128)}, f32[32,4,128]{2,1,0:T(4,128)S(1)}, /*index=5*/s32[]{:T(128)}) while((s32[]{:T(128)}, f32[16,4,128]{2,0,1:T(8,128)S(1)}, f32[16,4,128]{2,0,1:T(8,128)S(1)}, s32[8,16]{1,0:T(8,128)}, f32[32,4,128]{2,1,0:T(4,128)S(1)}, ...), condition=%wide.region_11.12_spmd, body=%wide.region_6.11_spmd.sunk | while | flops 5008434 | bytes 373073 | solution.py:75
  (195 shorter events, 95.1 us)
Async XLA Ops:
  0.0 2.4 %copy-start.3 = (s32[1,128]{1,0:T(1,128)S(1)}, s32[1,128]{1,0:T(1,128)}, u32[]{:S(2)}) copy-start(s32[1,128]{1,0:T(1,128)} %param.14) | copy-start | bytes 1540
  10.3 11.5 %copy-start.2 = (s32[1,4,4]{2,1,0:T(4,128)S(1)}, s32[1,4,4]{2,1,0:T(4,128)}, u32[]{:S(2)}) copy-start(s32[1,4,4]{2,1,0:T(4,128)} %param.15) | copy-start | bytes 196
  10.3 11.5 %copy-start = (f32[4,2048]{1,0:T(4,128)S(1)}, f32[4,2048]{1,0:T(4,128)}, u32[]{:S(2)}) copy-start(f32[4,2048]{1,0:T(4,128)} %param.11) | copy-start | bytes 98308
  10.3 23.8 %copy-start.1 = (s32[16,16]{1,0:T(8,128)S(1)}, s32[16,16]{1,0:T(8,128)}, u32[]{:S(2)}) copy-start(s32[16,16]{1,0:T(8,128)} %param.16) | copy-start | bytes 3076
  10.3 47.4 %all-to-all-start = ((f32[128,4,10,128]{3,1,2,0:T(4,128)}), f32[128,4,10,128]{3,1,2,0:T(4,128)S(1)}, u32[]{:S(2)}, u32[]{:S(2)}) async-start(f32[128,4,10,128]{3,1,2,0:T(4,128)} %copy_multiply_fusion), calls=%async_computation | async-start | bytes 5242880 | tf_op jit(solution)/shard_map/all_to_all | solution.py:80
  22.4 18.3 %collective-permute-start = (f32[4,4,128]{2,1,0:T(4,128)S(1)}, f32[4,4,128]{2,1,0:T(4,128)S(1)}, u32[]{:S(2)}, u32[]{:S(2)}) collective-permute-start(f32[4,4,128]{2,1,0:T(4,128)S(1)} %gather_fusion.3), channel_id=1, source_target_pairs={{0,1},{1,2},{2,3},{3,4},{4,5},{5,6},{6,7},{7,8},{8,9},{9,10},{10,1... | collective-permute-start | bytes 24584 | tf_op jit(solution)/shard_map/ppermute | solution.py:16
  26.6 22.1 %collective-permute-start.1 = (f32[4,4,128]{2,1,0:T(4,128)S(1)}, f32[4,4,128]{2,1,0:T(4,128)S(1)}, u32[]{:S(2)}, u32[]{:S(2)}) collective-permute-start(f32[4,4,128]{2,1,0:T(4,128)S(1)} %gather_fusion.4), channel_id=1, source_target_pairs={{1,0},{2,1},{3,2},{4,3},{5,4},{6,5},{7,6},{8,7},{9,8},{10,9},{11,1... | collective-permute-start | bytes 24584 | tf_op jit(solution)/shard_map/ppermute | solution.py:16
  29.1 19.6 %collective-permute-start.2 = (f32[4,4,128]{2,1,0:T(4,128)S(1)}, f32[4,4,128]{2,1,0:T(4,128)S(1)}, u32[]{:S(2)}, u32[]{:S(2)}) collective-permute-start(f32[4,4,128]{2,1,0:T(4,128)S(1)} %gather_fusion.5), channel_id=1, source_target_pairs={{0,2},{1,3},{2,4},{3,5},{4,6},{5,7},{6,8},{7,9},{8,10},{9,11},{10,... | collective-permute-start | bytes 24584 | tf_op jit(solution)/shard_map/ppermute | solution.py:16
  32.7 15.9 %collective-permute-start.3 = (f32[4,4,128]{2,1,0:T(4,128)S(1)}, f32[4,4,128]{2,1,0:T(4,128)S(1)}, u32[]{:S(2)}, u32[]{:S(2)}) collective-permute-start(f32[4,4,128]{2,1,0:T(4,128)S(1)} %gather_fusion.6), channel_id=1, source_target_pairs={{2,0},{3,1},{4,2},{5,3},{6,4},{7,5},{8,6},{9,7},{10,8},{11,9},{12,... | collective-permute-start | bytes 24584 | tf_op jit(solution)/shard_map/ppermute | solution.py:16
where the time goes:
time: 192 us; the launch traced here: 190 us
  other arithmetic  80.5 us (42%)
  local copies, waits for them, and re-layouts  63.3 us (33%)
  waiting for transfers between devices  23.5 us (12%)
  starting transfers between devices  21.3 us (11%)
    reduce_sum x16, other arithmetic, cell_tile(): accel_x = jnp.sum(radial * delta_x + quad_x * inv_five, axis=1)  49.4 us
    gather x16, local copies, waits for them, and re-layouts, add_cells(): return (total + cell_batch(target_blocks, cell_pool[column]), None)  46.3 us
    reduce_sum x8, other arithmetic, near_tile(): accel_x = jnp.sum(near_radial * near_x, axis=1)  18 us
    ppermute x4, waiting for transfers between devices, from_behind(): return lax.ppermute(block, axis, route)  14.5 us
    all_to_all x1, starting transfers between devices, exchange_cells(): lax.all_to_all(chosen, ('gx', 'gy'), split_axis=0, concat_axis=0, tiled=T...  11.5 us
    ppermute x4, starting transfers between devices, from_behind(): return lax.ppermute(block, axis, route)  9.82 us
    all_to_all x1, waiting for transfers between devices, exchange_cells(): lax.all_to_all(chosen, ('gx', 'gy'), split_axis=0, concat_axis=0, tiled=T...  9.06 us
    unnamed x17, local copies, waits for them, and re-layouts  5.82 us
  transfers between devices with their start and end apart: 5, of which 3 were waited for; matrix products, arithmetic and copies ran while one was open for 1% of the time, Pallas kernels for 0%

commit v1 on v0

v1 whole, which is shorter than its diff:
```python
import jax
import jax.numpy as jnp
from jax import lax
from jax.experimental import pallas as pl
from jax.experimental.pallas import tpu as pltpu
from jax.sharding import PartitionSpec as P

BLK = 128
NBLK = 16
NCB = 64
DEV = 128
LC = 16
LP = 8
ROWS = 9
EPS = 0.0025
MESH = pl.DeviceIdType.MESH
near_offsets = (1, -1, 2, -2)

ZERO = NCB + 2 * DEV
APOOL = ZERO + 1
NA = 9

f32 = jnp.float32
i32 = jnp.int32


def rows_of(ref, block, count):
    return [jnp.broadcast_to(ref[block, r], (8, BLK)) for r in range(count)]


def cell_item(t_ref, t_base, pool, block, acc):
    X, Y, Z, M, Qxx, Qyy, Qxy, Qxz, Qyz = rows_of(pool, block, ROWS)
    Qzz = -(Qxx + Qyy)

    def tile(t, carry):
        s = pl.ds(pl.multiple_of(t * 8, 8), 8)
        x = t_ref[t_base, s] - X
        y = t_ref[t_base + 1, s] - Y
        z = t_ref[t_base + 2, s] - Z
        u = lax.rsqrt(x * x + y * y + z * z + EPS)
        u2 = u * u
        qx = Qxx * x + Qxy * y + Qxz * z
        qy = Qxy * x + Qyy * y + Qyz * z
        qz = Qxz * x + Qyz * y + Qzz * z
        v = (x * qx + y * qy + z * qz) * (u2 * u2)
        u3 = u * u2
        p = u3 * (M + 2.5 * v)
        u5 = u3 * u2
        acc[0, s] += p * x - u5 * qx
        acc[1, s] += p * y - u5 * qy
        acc[2, s] += p * z - u5 * qz
        acc[3, s] += u * (M + 0.5 * v)
        return carry

    lax.fori_loop(0, 16, tile, 0, unroll=True)


def near_item(t_ref, t_base, pool, block, acc):
    X, Y, Z, M = rows_of(pool, block, 4)

    def tile(t, carry):
        s = pl.ds(pl.multiple_of(t * 8, 8), 8)
        x = t_ref[t_base, s] - X
        y = t_ref[t_base + 1, s] - Y
        z = t_ref[t_base + 2, s] - Z
        u = lax.rsqrt(x * x + y * y + z * z + EPS)
        mu = M * u
        p = mu * (u * u)
        acc[0, s] += p * x
        acc[1, s] += p * y
        acc[2, s] += p * z
        acc[3, s] += mu
        return carry

    lax.fori_loop(0, 16, tile, 0, unroll=True)


def lane_totals(acc):
    lane = lax.broadcasted_iota(i32, (BLK, BLK), 1)
    packed = jnp.zeros((BLK, BLK), f32)
    for k in range(4):
        total = jnp.sum(acc[k], axis=1, keepdims=True)
        packed = jnp.where(lane == k, jnp.broadcast_to(total, (BLK, BLK)), packed)
    return -jnp.transpose(packed)[:8]


def spread_targets(parts, t_ref, j, base):
    cols = jnp.transpose(parts[:, pl.ds(pl.multiple_of(j * BLK, BLK), BLK)])
    for c in range(3):
        t_ref[base + c] = jnp.broadcast_to(cols[:, c : c + 1], (BLK, BLK))


def exchange_kernel(
    let_list, let_count, part_list, near_lists, cell_lists, parts, cells,
    part_out, a_out, b_out,
    own_cells, own_rows, chosen_a, chosen_b, apool, npick, npool, t_ref, acc, list_v, list_s,
    send_a, recv_a, send_b, recv_b, send_n, recv_n, local_sem,
):
    gx = lax.axis_index("gx")
    gy = lax.axis_index("gy")
    me = gx * 8 + gy
    cx, cz = gx // 4, lax.rem(gx, 4)
    cy, cc = gy // 2, lax.rem(gy, 2)

    barrier = pltpu.get_barrier_semaphore()

    def greet(i, carry):
        d = lax.rem(me + i, DEV)
        pl.semaphore_signal(
            barrier, inc=1, device_id=(d // 8, lax.rem(d, 8)), device_id_type=MESH
        )
        return carry

    lax.fori_loop(1, DEV, greet, 0)

    order = (0, 1, 2, 3, 4, 5, 7, 8, 9)

    def own_block(b, carry):
        at = pl.ds(pl.multiple_of(b * BLK, BLK), BLK)
        for r, source in enumerate(order):
            row = cells[source : source + 1, at]
            own_cells[b, r] = row
            apool[b, r] = row
        return carry

    lax.fori_loop(0, NCB, own_block, 0)
    for r in range(ROWS):
        apool[ZERO, r] = jnp.zeros((1, BLK), f32)

    def own_parts(b, carry):
        at = pl.ds(pl.multiple_of(b * BLK, BLK), BLK)
        for r in range(4):
            row = parts[r : r + 1, at]
            own_rows[b, r] = row
            npool[b, r] = row
        return carry

    lax.fori_loop(0, NBLK, own_parts, 0)

    for position, offset in enumerate(near_offsets):
        target = me + offset
        keep = jnp.where((target >= 0) & (target < DEV), 1.0, 0.0).astype(f32)
        for b in range(4):
            pick = own_rows[part_list[position * 4 + b]]
            npick[position * 4 + b] = pick * keep

    def choose(d, carry):
        count = let_count[d]
        for k in range(4):
            live = jnp.where(k < count, 1.0, 0.0).astype(f32)
            block = own_cells[let_list[d * 4 + k]] * live
            if k < 2:
                chosen_a[d * 2 + k] = block
            else:
                chosen_b[d * 2 + k - 2] = block
        return carry

    lax.fori_loop(0, DEV, choose, 0)

    ids = cell_lists[...]
    lane = lax.broadcasted_iota(i32, (NBLK, BLK), 1)
    remote = ids - NCB
    slot = remote & 3
    early = ((ids < NCB) | (slot < 2)) & (lane < LC)
    place = jnp.where(ids < NCB, ids, NCB + 2 * (remote >> 2) + slot)
    rank = early.astype(i32)
    for shift in (1, 2, 4, 8):
        rank = rank + jnp.where(lane >= shift, pltpu.roll(rank, shift, 1), 0)
    packed = jnp.full((NBLK, BLK), ZERO, i32)
    for p in range(NA):
        hit = jnp.where(early & (rank == p + 1), ZERO - place, 0)
        found = jnp.sum(hit, axis=1, keepdims=True)
        packed = jnp.where(lane == p, ZERO - found, packed)
    list_v[...] = packed
    to_smem = pltpu.make_async_copy(list_v, list_s, local_sem)
    to_smem.start()
    to_smem.wait()

    def spread(j, carry):
        spread_targets(parts, t_ref, j, j * 3)
        return carry

    lax.fori_loop(0, NBLK, spread, 0)

    pl.semaphore_wait(barrier, DEV - 1)

    for position, offset in enumerate(near_offsets):
        d = lax.rem(me + offset + DEV, DEV)
        pltpu.make_async_remote_copy(
            npick.at[pl.ds(position * 4, 4)],
            npool.at[pl.ds(NBLK + position * 4, 4)],
            send_n.at[position],
            recv_n.at[position],
            device_id=(d // 8, lax.rem(d, 8)),
            device_id_type=MESH,
        ).start()

    def send_pairs(chosen, pool, base, send, recv):
        def send_one(i, carry):
            dx = lax.rem(i, 4)
            dy = lax.rem(i // 4 + dx, 4)
            dz = lax.rem(i // 16 + 2 * dx + dy, 4)
            ngx = lax.rem(cx + dx, 4) * 4 + lax.rem(cz + dz, 4)
            ngy = lax.rem(cy + dy, 4) * 2 + lax.rem(cc + i // 64, 2)
            d = ngx * 8 + ngy
            pltpu.make_async_remote_copy(
                chosen.at[pl.ds(d * 2, 2)],
                pool.at[pl.ds(base + me * 2, 2)],
                send,
                recv,
                device_id=(ngx, ngy),
                device_id_type=MESH,
            ).start()
            return carry

        lax.fori_loop(1, DEV, send_one, 0)

    def pair_wait(chosen, pool, base, send, recv):
        pltpu.make_async_remote_copy(
            chosen.at[pl.ds(0, 2 * DEV - 2)],
            pool.at[pl.ds(base, 2 * DEV - 2)],
            send,
            recv,
            device_id=(gx, gy),
            device_id_type=MESH,
        ).wait()

    send_pairs(chosen_a, apool, NCB, send_a, recv_a)
    send_pairs(chosen_b, b_out, 0, send_b, recv_b)
    own_a = pltpu.make_async_copy(
        chosen_a.at[pl.ds(me * 2, 2)], apool.at[pl.ds(NCB + me * 2, 2)], local_sem
    )
    own_a.start()
    own_a.wait()
    own_b = pltpu.make_async_copy(
        chosen_b.at[pl.ds(me * 2, 2)], b_out.at[pl.ds(me * 2, 2)], local_sem
    )
    own_b.start()
    own_b.wait()

    for position in range(4):
        pltpu.make_async_remote_copy(
            npick.at[pl.ds(position * 4, 4)],
            npool.at[pl.ds(NBLK + position * 4, 4)],
            send_n.at[position],
            recv_n.at[position],
            device_id=(gx, gy),
            device_id_type=MESH,
        ).wait()

    def near_block(j, carry):
        acc[j] = jnp.zeros((4, BLK, BLK), f32)

        def item(i, inner):
            near_item(t_ref, j * 3, npool, near_lists[j * LP + i], acc.at[j])
            return inner

        lax.fori_loop(0, LP, item, 0)
        return carry

    lax.fori_loop(0, NBLK, near_block, 0)

    pair_wait(chosen_a, apool, NCB, send_a, recv_a)
    keep_a = pltpu.make_async_copy(apool, a_out, local_sem)
    keep_a.start()

    def cell_block(j, carry):
        def item(i, inner):
            cell_item(t_ref, j * 3, apool, list_s[j, i], acc.at[j])
            return inner

        lax.fori_loop(0, NA, item, 0)
        part_out[j] = lane_totals(acc.at[j])
        return carry

    lax.fori_loop(0, NBLK, cell_block, 0)

    keep_a.wait()
    pair_wait(chosen_b, b_out, 0, send_b, recv_b)


def rest_kernel(
    cell_lists, parts, partial, a_in, b_in, out,
    pool, t_ref, acc, live_v, live_s, items, sem,
):
    copy_a = pltpu.make_async_copy(a_in, pool.at[pl.ds(0, APOOL)], sem.at[0])
    copy_b = pltpu.make_async_copy(b_in, pool.at[pl.ds(APOOL, 2 * DEV)], sem.at[1])
    copy_a.start()
    copy_b.start()
    copy_b.wait()
    masses = pool[pl.ds(APOOL, 2 * DEV), 3].reshape(2 * DEV, BLK)
    for h in range(2):
        flipped = jnp.transpose(masses[h * DEV : (h + 1) * DEV])
        live_v[h : h + 1] = (flipped[:1] > 0).astype(i32)
    to_smem = pltpu.make_async_copy(live_v, live_s, sem.at[1])
    to_smem.start()
    to_smem.wait()
    copy_a.wait()

    def block(j, carry):
        acc[...] = jnp.zeros((4, BLK, BLK), f32)
        spread_targets(parts, t_ref, j, 0)

        def pick(i, state):
            rank, n = state
            c = cell_lists[j * LC + i]
            own = c < NCB
            remote = jnp.where(own, 0, c - NCB)
            slot = remote & 3
            sender = remote >> 2
            early = own | (slot < 2)
            late = jnp.where(early, 0, sender * 2 + slot - 2)
            live = live_s[late >> 7, late & 127]
            rank = rank + early.astype(i32)
            todo = jnp.where(early, (rank > NA).astype(i32), live)
            place = jnp.where(own, c, NCB + 2 * sender + slot)
            items[n] = jnp.where(early, place, APOOL + late)
            return rank, n + todo

        rank, n = lax.fori_loop(0, LC, pick, (jnp.int32(0), jnp.int32(0)))

        def item(i, inner):
            cell_item(t_ref, 0, pool, items[i], acc)
            return inner

        lax.fori_loop(0, n, item, 0)
        total = lane_totals(acc) + partial[j]
        out[:, pl.ds(pl.multiple_of(j * BLK, BLK), BLK)] = total[:4]
        return carry

    lax.fori_loop(0, NBLK, block, 0)


def body(particles, tree_cells, let_list, let_count, part_list, cell_lists, near_lists):
    smem = pl.BlockSpec(memory_space=pltpu.SMEM)
    vmem = pl.BlockSpec(memory_space=pltpu.VMEM)
    hbm = pl.BlockSpec(memory_space=pl.ANY)
    block = (ROWS, 1, BLK)
    padded = jnp.pad(cell_lists, ((0, 0), (0, BLK - LC)))
    partial, a_pool, b_pool = pl.pallas_call(
        exchange_kernel,
        out_shape=(
            jax.ShapeDtypeStruct((NBLK, 8, BLK), f32),
            jax.ShapeDtypeStruct((APOOL, *block), f32),
            jax.ShapeDtypeStruct((2 * DEV, *block), f32),
        ),
        in_specs=[smem] * 4 + [vmem] * 3,
        out_specs=(vmem, hbm, hbm),
        scratch_shapes=[
            pltpu.VMEM((NCB, *block), f32),
            pltpu.VMEM((NBLK, 4, 1, BLK), f32),
            pltpu.VMEM((2 * DEV, *block), f32),
            pltpu.VMEM((2 * DEV, *block), f32),
            pltpu.VMEM((APOOL, *block), f32),
            pltpu.VMEM((16, 4, 1, BLK), f32),
            pltpu.VMEM((2 * NBLK, 4, 1, BLK), f32),
            pltpu.VMEM((3 * NBLK, BLK, BLK), f32),
            pltpu.VMEM((NBLK, 4, BLK, BLK), f32),
            pltpu.VMEM((NBLK, BLK), i32),
            pltpu.SMEM((NBLK, BLK), i32),
            pltpu.SemaphoreType.DMA,
            pltpu.SemaphoreType.DMA,
            pltpu.SemaphoreType.DMA,
            pltpu.SemaphoreType.DMA,
            pltpu.SemaphoreType.DMA((4,)),
            pltpu.SemaphoreType.DMA((4,)),
            pltpu.SemaphoreType.DMA,
        ],
        compiler_params=pltpu.CompilerParams(
            collective_id=0, has_side_effects=True, vmem_limit_bytes=60 << 20
        ),
        name="exchange",
    )(
        let_list.reshape(-1), let_count.reshape(-1), part_list.reshape(-1),
        near_lists.reshape(-1), padded, particles, tree_cells,
    )
    return pl.pallas_call(
        rest_kernel,
        out_shape=jax.ShapeDtypeStruct(particles.shape, f32),
        in_specs=[smem, vmem, vmem, hbm, hbm],
        out_specs=vmem,
        scratch_shapes=[
            pltpu.VMEM((APOOL + 2 * DEV, *block), f32),
            pltpu.VMEM((3, BLK, BLK), f32),
            pltpu.VMEM((4, BLK, BLK), f32),
            pltpu.VMEM((8, BLK), i32),
            pltpu.SMEM((8, BLK), i32),
            pltpu.SMEM((LC + 1,), i32),
            pltpu.SemaphoreType.DMA((2,)),
        ],
        compiler_params=pltpu.CompilerParams(vmem_limit_bytes=60 << 20),
        name="rest",
    )(cell_lists.reshape(-1), particles, partial, a_pool, b_pool)


def solution(mesh):
    return jax.shard_map(
        body,
        mesh=mesh,
        in_specs=(
            P(None, ("gx", "gy")),
            P(None, ("gx", "gy")),
            P(("gx", "gy"), None, None),
            P(("gx", "gy"), None),
            P(("gx", "gy"), None, None),
            P(("gx", "gy"), None),
            P(("gx", "gy"), None),
        ),
        out_specs=P(None, ("gx", "gy")),
        check_vma=False,
    )
```

time: 192 us -> 87.7 us (0.46)
  Pallas kernels: 0 us -> 80.6 us
  other arithmetic: 80.5 us -> 0 us
  local copies, waits for them, and re-layouts: 63.3 us -> 6.85 us
  waiting for transfers between devices: 23.5 us -> 0 us
  starting transfers between devices: 21.3 us -> 0 us
    pallas_call x0 -> x2, Pallas kernels: none -> 80.6 us  [the longest x1 58.2 us: body(): pl.pallas_call(exchange_kernel, out_shape=(jax.ShapeDtypeStruct((NBLK, 8,...]
    reduce_sum x24 -> x0, other arithmetic: 67.4 us -> none  [the longest x16 49.4 us: cell_tile(): accel_x = jnp.sum(radial * delta_x + quad_x * inv_five, axis=1)]
    gather x29 -> x0, local copies, waits for them, and re-layouts: 56.3 us -> none  [the longest x16 46.3 us: add_cells(): return (total + cell_batch(target_blocks, cell_pool[column]), None)]
    ppermute x4 -> x0, waiting for transfers between devices: 14.5 us -> none  [from_behind(): return lax.ppermute(block, axis, route)]
    all_to_all x1 -> x0, starting transfers between devices: 11.5 us -> none  [exchange_cells(): lax.all_to_all(chosen, ('gx', 'gy'), split_axis=0, concat_axis=0, tiled=T...]
    ppermute x4 -> x0, starting transfers between devices: 9.82 us -> none  [from_behind(): return lax.ppermute(block, axis, route)]
    all_to_all x1 -> x0, waiting for transfers between devices: 9.06 us -> none  [exchange_cells(): lax.all_to_all(chosen, ('gx', 'gy'), split_axis=0, concat_axis=0, tiled=T...]
    select_n x26 -> x0, other arithmetic: 6.45 us -> none  [the longest x8 5.58 us: add_near(): return (total + near_batch(target_blocks, near_pool[column]), None)]
  transfers between devices with their start and end apart: 5 -> 0, of which waited for: 3 -> 0; matrix products, arithmetic and copies ran while one was open for 1% -> 0% of each run, Pallas kernels for 0% -> 0%
where the time goes in v1:
time: 87.7 us; the launch traced here: 87.4 us
  Pallas kernels  80.6 us (92%)
  local copies, waits for them, and re-layouts  6.85 us (8%)
    pallas_call x1, Pallas kernels, body(): pl.pallas_call(exchange_kernel, out_shape=(jax.ShapeDtypeStruct((NBLK, 8,...  58.2 us
    pallas_call x1, Pallas kernels, body(): pl.pallas_call(rest_kernel, out_shape=jax.ShapeDtypeStruct(particles.shap...  22.4 us

profile of v1, /device:TPU:1, one launch (start us, length us, event | category | flops | bytes accessed | tf_op | source)
XLA Modules:
  0.0 87.4 jit_solution(2956557398982704729)
XLA Ops:
  0.0 1.4 %reshape.18.part_list = s32[16]{0:T(128)} reshape(s32[1,4,4]{2,1,0:T(4,128)} %param.11) | data formatting | bytes 128 | tf_op jit(solution)/shard_map/reshape | solution.py:374
  1.4 1.4 %reshape.15.cell_lists = s32[256]{0:T(256)} reshape(s32[16,16]{1,0:T(8,128)} %param.12) | data formatting | bytes 2048 | tf_op jit(solution)/shard_map/reshape | solution.py:393
  2.7 0.8 copy.10
  3.5 0.6 reshape.19.near_lists
  4.1 1.3 %pad.4.cell_lists = s32[16,128]{1,0:T(8,128)} pad(s32[16,16]{1,0:T(8,128)} %param.12, s32[]{:T(128)} %constant.0.clone.1), padding=0_0x0_112 | pad | bytes 9220 | tf_op jit(solution)/shard_map/jit(_pad)/pad | solution.py:339
  5.4 0.8 copy.9
  6.2 0.7 reshape.16.let_list
  6.9 58.2 %exchange.1 = (f32[16,8,128]{2,1,0:T(8,128)}, f32[321,9,1,128]{3,2,1,0:T(1,128)}, f32[256,9,1,128]{3,2,1,0:T(1,128)}) custom-call(s32[512]{0:T(512)} %reshape.16.let_list, s32[128]{0:T(128)} %bitcast.1, s32[16]{0:T(128)} %reshape.18.part_list, s32[128]{0:T(128)} %reshape.19.near_lists, s32[16,128]{1,0:T(8,128)} %pad.4.cell_lists, f32[4,2048]{1,0:T(4,128)} %parts.3, ...), custom_call_target="tpu_custom_call" | custom-call | tf_op jit(solution)/shard_map/exchange/pallas_call | solution.py:340
  65.0 22.4 %rest.1 = f32[4,2048]{1,0:T(4,128)} custom-call(s32[256]{0:T(256)} %reshape.15.cell_lists, f32[4,2048]{1,0:T(4,128)} %parts.3, f32[16,8,128]{2,1,0:T(8,128)} %get-tuple-element.8.partial, f32[321,9,1,128]{3,2,1,0:T(1,128)} %get-tuple-element.9.a_in, f32[256,9,1,128]{3,2,1,0:T(1,128)} %get-tuple-element.10.b_in), custom_call_target="tpu_custom_call" | custom-call | tf_op jit(solution)/shard_map/rest/pallas_call | solution.py:377
